TPU v7x, 32 devices: a whole 2x2x4 slice. The times are simulated.
32 devices in a mesh: tok: 4 (over z), hid: 8 (over y, x, core).
Axes of the slice: x: 2, y: 2, z: 4, core: 2. Of those that a mesh axis runs over, the one named last changes fastest.
Arguments:
- tokens: bfloat16 [2048, 1024], P('tok', 'hid'), may hold values from -6 to 6
- cotangent: bfloat16 [2048, 1024], P('tok', 'hid'), may hold values from -6 to 6
- frozen_in: bfloat16 [1024, 16384], P('tok', 'hid'), may hold values from -0.1875 to 0.1875
- frozen_out: bfloat16 [16384, 1024], P('hid', 'tok'), may hold values from -0.046875 to 0.046875
- input_adapter_first: bfloat16 [1024, 128], P('hid'), may hold values from -0.1875 to 0.1875
- input_adapter_second: bfloat16 [128, 16384], P(None, 'hid'), may hold values from -0.5 to 0.5
- adapter_out_a: bfloat16 [16384, 128], P('hid'), may hold values from -0.046875 to 0.046875
- adapter_out_b: bfloat16 [128, 1024], replicated, may hold values from -0.5 to 0.5
Outputs:
- input_gradient: float32 [2048, 1024], P('tok', 'hid')
- grad_in_a: float32 [1024, 128], P('hid')
- grad_in_b: float32 [128, 16384], P(None, 'hid')
- grad_out_a: float32 [16384, 128], P('hid')
- grad_out_b: float32 [128, 1024], P(None, 'hid')
All inputs are finite; a program needn't handle non-finite values.
Results may differ from a plain program's by a relative error of at most 0.0029.
Values may be sent and summed in bfloat16 or wider, within the bound.
A program may use at most 64 MiB of HBM per device.

v0:
```python
import math
import jax
import jax.numpy as jnp
from jax import lax
from jax.sharding import PartitionSpec as P

ADAPTER_SCALE = 0.5
GELU_K = 0.7978845608
GELU_C = 0.044715


def gelu_pair(pre_activation):
    tangent = jnp.tanh(
        GELU_K * (pre_activation + GELU_C * pre_activation * pre_activation * pre_activation)
    )
    value_out = 0.5 * pre_activation * (1.0 + tangent)
    slopes = 0.5 * (1.0 + tangent) + 0.5 * pre_activation * (1.0 - tangent * tangent) * GELU_K * (
        1.0 + 3.0 * GELU_C * pre_activation * pre_activation
    )
    return (value_out, slopes)


def local(
    tokens,
    cotangent,
    frozen_in,
    frozen_out,
    input_adapter_first,
    input_adapter_second,
    adapter_out_a,
    adapter_out_b,
):
    highest_precision = lax.Precision.HIGHEST
    device_local_rows = tokens.shape[0]
    rank_width = input_adapter_second.shape[0]
    gradient_scale = ADAPTER_SCALE / math.sqrt(device_local_rows * lax.axis_size("tok"))
    full_tokens, full_cotan = (
        lax.all_gather(tokens, "hid", axis=1, tiled=True),
        lax.all_gather(cotangent, "hid", axis=1, tiled=True),
    )
    in_rows = lax.all_gather(frozen_in, "tok", axis=0, tiled=True)
    in_a_full = lax.all_gather(input_adapter_first, "hid", axis=0, tiled=True)
    lowrank_input = jnp.dot(full_tokens, in_a_full, preferred_element_type=jnp.float32)
    second_float = input_adapter_second.astype(jnp.float32)
    out_a_float = adapter_out_a.astype(jnp.float32)
    pre_activation = jnp.dot(
        full_tokens, in_rows, preferred_element_type=jnp.float32
    ) + ADAPTER_SCALE * jnp.dot(lowrank_input, second_float, precision=highest_precision)
    value_out, slopes = gelu_pair(pre_activation)
    hidden_act = value_out.astype(jnp.bfloat16)
    backward_lowrank = jnp.einsum(
        "td,rd->tr", full_cotan, adapter_out_b, preferred_element_type=jnp.float32
    )
    rank_out = jnp.dot(hidden_act, adapter_out_a, preferred_element_type=jnp.float32)
    dense_backward = jnp.einsum(
        "td,fd->tf",
        full_cotan,
        lax.all_gather(frozen_out, "tok", axis=1, tiled=True),
        preferred_element_type=jnp.float32,
    )
    dense_backward = dense_backward + ADAPTER_SCALE * jnp.dot(
        backward_lowrank, out_a_float.T, precision=highest_precision
    )
    grad_pre = (dense_backward * slopes).astype(jnp.bfloat16)
    rank_backward = jnp.einsum(
        "tf,rf->tr", grad_pre, input_adapter_second, preferred_element_type=jnp.float32
    )
    dense_in = jnp.einsum("tf,df->td", grad_pre, in_rows, preferred_element_type=jnp.float32)
    grad_out_a = gradient_scale * jnp.dot(
        hidden_act.astype(jnp.float32).T, backward_lowrank, precision=highest_precision
    )
    grad_in_b = gradient_scale * jnp.dot(
        lowrank_input.T, grad_pre.astype(jnp.float32), precision=highest_precision
    )
    in_a_float = in_a_full.astype(jnp.float32)
    dx_term = dense_in + ADAPTER_SCALE * jnp.dot(
        rank_backward, in_a_float.T, precision=highest_precision
    )
    out_term = jnp.dot(rank_out.T, full_cotan.astype(jnp.float32), precision=highest_precision)
    in_term = jnp.dot(rank_backward.T, full_tokens.astype(jnp.float32), precision=highest_precision)
    rank_terms = jnp.concatenate([out_term, in_term], axis=0)
    input_gradient, rank_local = (
        lax.psum_scatter(dx_term, "hid", scatter_dimension=1, tiled=True),
        lax.psum_scatter(rank_terms, "hid", scatter_dimension=1, tiled=True),
    )
    grad_out_a, grad_in_b, rank_total = lax.psum((grad_out_a, grad_in_b, rank_local), "tok")
    grad_out_b = gradient_scale * rank_total[:rank_width]
    grad_in_a = gradient_scale * rank_total[rank_width:].T
    return (input_gradient, grad_in_a, grad_in_b, grad_out_a, grad_out_b)


def solution(mesh):
    in_specs = (
        P("tok", "hid"),
        P("tok", "hid"),
        P("tok", "hid"),
        P("hid", "tok"),
        P("hid", None),
        P(None, "hid"),
        P("hid", None),
        P(),
    )
    out_specs = (P("tok", "hid"), P("hid", None), P(None, "hid"), P("hid", None), P(None, "hid"))
    return jax.shard_map(local, mesh=mesh, in_specs=in_specs, out_specs=out_specs, check_vma=False)
```

profile of v0, /device:TPU:0, one launch (start us, length us, event | category | flops | bytes accessed | tf_op | source)
XLA Modules:
  0.0 421.3 jit_solution(1950593718763780741)
XLA Ops:
  7.2 0.0 copy-start
  7.2 0.0 all-gather.5.cloned.1.call-start
  7.2 0.7 all-gather.5.cloned.1.call-update
  7.9 0.0 all-gather.9.cloned.1.call-start
  8.0 0.7 all-gather.9.cloned.1.call-update
  8.7 0.0 all-gather.11.cloned.1.call-start
  8.7 0.7 all-gather.11.cloned.1.call-update
  9.4 0.0 all-gather.7.cloned.1.call-start
  9.4 0.5 all-gather.7.cloned.1.call-update
  10.0 0.0 reduce-scatter.5.cloned.1.call-start
  10.0 11.0 %all_gather.19 = bf16[1024,128]{1,0:T(8,128)(2,1)S(1)} all-gather(bf16[128,128]{1,0:T(8,128)(2,1)} %param.12), channel_id=1, replica_groups=mesh['tok'=4,'hid'=8] {'hid'}, dimensions={0}, use_global_device_ids=true | all-gather | bytes 294912 | tf_op jit(solution)/shard_map/all_gather | solution.py:42
  21.0 15.1 %all-gather.5.cloned.1.call-done = bf16[512,1024]{1,0:T(8,128)(2,1)} async-done(((bf16[512,128]{1,0:T(8,128)(2,1)}), bf16[512,1024]{1,0:T(8,128)(2,1)}) %all-gather.5.cloned.1.call-update) | async-done | bytes 1048592 | tf_op jit(solution)/shard_map/all_gather | solution.py:39
  36.1 1.7 fusion.9
  37.8 23.7 %all-gather.9.cloned.1.call-done = bf16[512,1024]{1,0:T(8,128)(2,1)} async-done(((bf16[512,128]{1,0:T(8,128)(2,1)}), bf16[512,1024]{1,0:T(8,128)(2,1)}) %all-gather.9.cloned.1.call-update) | async-done | bytes 1048592 | tf_op jit(solution)/shard_map/all_gather | solution.py:38
  61.5 1.7 fusion.11
  63.1 0.0 copy-start.6
  63.2 80.7 %all-gather.11.cloned.1.call-done = bf16[1024,2048]{1,0:T(8,128)(2,1)} async-done(((bf16[256,2048]{1,0:T(8,128)(2,1)}), bf16[1024,2048]{1,0:T(8,128)(2,1)}) %all-gather.11.cloned.1.call-update) | async-done | bytes 4194320 | tf_op jit(solution)/shard_map/all_gather | solution.py:41
  143.8 4.8 %fusion.10 = f32[512,2048]{1,0:T(8,128)S(1)} fusion(bf16[512,1024]{1,0:T(8,128)(2,1)} %all-gather.9.cloned.1.call-done, bf16[1024,2048]{1,0:T(8,128)(2,1)} %all-gather.11.cloned.1.call-done), kind=kOutput, calls=%fused_computation.20 | convolution fusion | flops 2147483648 | bytes 9437184 | tf_op jit(solution)/shard_map/dot_general | solution.py:46
  148.7 0.0 copy-done.6
  148.7 0.0 copy-done
  148.7 0.0 copy-start.3
  148.7 5.9 %multiply_convert_fusion = (bf16[512,2048]{1,0:T(8,128)(2,1)}, f32[512,2048]{1,0:T(8,128)}) fusion(f32[512,2048]{1,0:T(8,128)S(1)} %fusion.10, f32[512,128]{1,0:T(8,128)S(1)} %fusion.11, bf16[128,2048]{1,0:T(8,128)(2,1)S(1)} %copy-done), kind=kOutput, calls=%fused_computation.9 | convolution fusion | flops 1622147072 | bytes 11272192 | tf_op jit(solution)/shard_map/dot_general | solution.py:48
  154.6 69.7 %all-gather.7.cloned.1.call-done = bf16[2048,1024]{1,0:T(8,128)(2,1)} async-done(((bf16[2048,256]{1,0:T(8,128)(2,1)}), bf16[2048,1024]{1,0:T(8,128)(2,1)}) %all-gather.7.cloned.1.call-update) | async-done | bytes 4194320 | tf_op jit(solution)/shard_map/all_gather | solution.py:58
  224.3 0.0 copy-done.3
  224.3 4.7 %fusion.8 = f32[512,2048]{1,0:T(8,128)S(1)} fusion(bf16[512,1024]{1,0:T(8,128)(2,1)S(1)} %copy-done.3, bf16[2048,1024]{1,0:T(8,128)(2,1)} %all-gather.7.cloned.1.call-done), kind=kOutput, calls=%fused_computation.18 | convolution fusion | flops 2147483648 | bytes 9437184 | tf_op jit(solution)/shard_map/td,fd->tf/dot_general | solution.py:55
  229.0 0.0 copy-done.7
  229.1 5.1 %fusion.6 = bf16[512,2048]{1,0:T(8,128)(2,1)S(1)} fusion(f32[512,2048]{1,0:T(8,128)S(1)} %copy-done.8, f32[512,2048]{1,0:T(8,128)S(1)} %fusion.8, f32[512,128]{1,0:T(8,128)S(1)} %fusion.9, bf16[2048,128]{1,0:T(8,128)(2,1)S(1)} %copy-done.7), kind=kOutput, calls=%fused_computation.8 | convolution fusion | flops 1632632832 | bytes 11272192 | tf_op jit(solution)/shard_map/dot_general | solution.py:61
  234.1 0.7 fusion.13
  234.9 0.7 fusion.14
  235.6 0.7 fusion.16
  236.3 0.7 fusion.15
  236.9 1.1 pad_maximum_fusion
  238.0 0.0 reduce-scatter.5.cloned.1.call-update
  238.0 0.0 all-reduce.3.cloned.1.call-start
  238.1 3.1 convolution_multiply_fusion.1
  241.2 3.3 convolution_multiply_fusion
  244.5 27.9 %reduce-scatter.5.cloned.1.call-done = f32[256,128]{1,0:T(8,128)} async-done(((f32[256,1024]{1,0:T(8,128)}), f32[256,128]{1,0:T(8,128)}) %reduce-scatter.5.cloned.1.call-update) | async-done | bytes 131088 | tf_op jit(solution)/shard_map/reduce_scatter | solution.py:84
  272.4 0.0 all-reduce.3.cloned.1.call-update
  272.4 0.0 reduce-scatter.3.cloned.1.call-start
  272.4 4.5 %fusion.12 = f32[512,1024]{1,0:T(8,128)S(1)} fusion(bf16[512,2048]{1,0:T(8,128)(2,1)S(1)} %fusion.6, bf16[1024,2048]{1,0:T(8,128)(2,1)} %all-gather.11.cloned.1.call-done), kind=kOutput, calls=%fused_computation.22 | convolution fusion | flops 2147483648 | bytes 8388608 | tf_op jit(solution)/shard_map/tf,df->td/dot_general | solution.py:68
  277.0 2.4 multiply_add_fusion.2
  279.4 0.0 reduce-scatter.3.cloned.1.call-update
  279.4 86.5 %all-reduce.3.cloned.1.call-done = (f32[256,128]{1,0:T(8,128)}, f32[128,2048]{1,0:T(8,128)}, f32[2048,128]{1,0:T(8,128)}) async-done(((f32[256,128]{1,0:T(8,128)}, f32[128,2048]{1,0:T(8,128)}, f32[2048,128]{1,0:T(8,128)}), (f32[256,128]{1,0:T(8,128)}, f32[128,2048]{1,0:T(8,128)}, f32[2048,128]{1,0:T(8,128)})) %all-reduce.3.cloned.1.call-update) | async-done | bytes 2228240 | tf_op jit(solution)/shard_map/psum | solution.py:86
  365.8 1.5 slice_multiply_fusion
  367.4 0.7 copy.13
  368.1 41.8 %reduce-scatter.3.cloned.1.call-done = f32[512,128]{1,0:T(8,128)} async-done(((f32[512,1024]{1,0:T(8,128)}), f32[512,128]{1,0:T(8,128)}) %reduce-scatter.3.cloned.1.call-update) | async-done | bytes 262160 | tf_op jit(solution)/shard_map/reduce_scatter | solution.py:83
  409.9 2.3 copy.17
  412.2 2.3 copy.18
  (11 shorter events, 0.0 us)
Async XLA Ops:
  7.2 141.5 %copy-start = (bf16[128,2048]{1,0:T(8,128)(2,1)S(1)}, bf16[128,2048]{1,0:T(8,128)(2,1)}, u32[]{:S(2)}) copy-start(bf16[128,2048]{1,0:T(8,128)(2,1)} %param.13) | copy-start | bytes 1572868
  7.2 28.9 %all-gather.5.cloned.1.call-start = ((), (), s32[]{:S(2)}) async-start(), calls=%async_computation.2 | async-start | bytes 1179648 | tf_op jit(solution)/shard_map/all_gather | solution.py:39
  7.9 53.6 %all-gather.9.cloned.1.call-start = ((), (), s32[]{:S(2)}) async-start(), calls=%async_computation.4 | async-start | bytes 1179648 | tf_op jit(solution)/shard_map/all_gather | solution.py:38
  8.7 135.2 %all-gather.11.cloned.1.call-start = ((), (), s32[]{:S(2)}) async-start(), calls=%async_computation.5 | async-start | bytes 5242880 | tf_op jit(solution)/shard_map/all_gather | solution.py:41
  9.4 214.9 %all-gather.7.cloned.1.call-start = ((), (), s32[]{:S(2)}) async-start(), calls=%async_computation.3 | async-start | bytes 5242880 | tf_op jit(solution)/shard_map/all_gather | solution.py:58
  10.0 262.4 %reduce-scatter.5.cloned.1.call-start = ((), (), s32[]{:S(2)}) async-start(), calls=%async_computation.7 | async-start | bytes 1179648 | tf_op jit(solution)/shard_map/reduce_scatter | solution.py:84
  63.1 85.5 %copy-start.6 = (f32[512,128]{1,0:T(8,128)}, f32[512,128]{1,0:T(8,128)S(1)}, u32[]{:S(2)}) copy-start(f32[512,128]{1,0:T(8,128)S(1)} %fusion.11) | copy-start | bytes 786436
  148.7 75.6 %copy-start.3 = (bf16[512,1024]{1,0:T(8,128)(2,1)S(1)}, bf16[512,1024]{1,0:T(8,128)(2,1)}, u32[]{:S(2)}) copy-start(bf16[512,1024]{1,0:T(8,128)(2,1)} %all-gather.5.cloned.1.call-done) | copy-start | bytes 3145732
  224.3 4.7 %copy-start.7 = (bf16[2048,128]{1,0:T(8,128)(2,1)S(1)}, bf16[2048,128]{1,0:T(8,128)(2,1)}, u32[]{:S(2)}) copy-start(bf16[2048,128]{1,0:T(8,128)(2,1)} %param.14) | copy-start | bytes 1572868
  224.3 4.7 %copy-start.8 = (f32[512,2048]{1,0:T(8,128)S(1)}, f32[512,2048]{1,0:T(8,128)}, u32[]{:S(2)}) copy-start(f32[512,2048]{1,0:T(8,128)} %get-tuple-element.16) | copy-start | bytes 12582916
  229.0 5.8 %copy-start.1 = (bf16[512,2048]{1,0:T(8,128)(2,1)S(1)}, bf16[512,2048]{1,0:T(8,128)(2,1)}, u32[]{:S(2)}) copy-start(bf16[512,2048]{1,0:T(8,128)(2,1)} %get-tuple-element.15) | copy-start | bytes 6291460
  234.1 1.5 copy-start.5
  234.1 2.1 copy-start.4
  238.0 127.8 %all-reduce.3.cloned.1.call-start = ((), (), s32[]{:S(2)}) async-start(), calls=%async_computation.8 | async-start | bytes 4456448 | tf_op jit(solution)/shard_map/psum | solution.py:86
  238.1 3.1 copy-start.2
  272.4 137.5 %reduce-scatter.3.cloned.1.call-start = ((), (), s32[]{:S(2)}) async-start(), calls=%async_computation.6 | async-start | bytes 2359296 | tf_op jit(solution)/shard_map/reduce_scatter | solution.py:83
Sparse Core Ops, SparseCore 0:
  9.9 26.1 all-gather.4
  38.0 23.4 all-gather.8
  63.1 80.7 all-gather.10
  145.2 79.0 all-gather.6
  238.1 34.1 reduce-scatter.4
  275.4 90.4 all-reduce.2
  369.7 40.1 reduce-scatter.2
where the time goes:
time: 422 us; the launch traced here: 421 us
  waiting for transfers between devices  348 us (82%)
  matrix products  39.9 us (9%)
  between operations  14.3 us (3%)
  blocking collectives  11 us (3%)
  local copies, waits for them, and re-layouts  5.33 us (1%)
    psum x1, waiting for transfers between devices, local(): lax.psum((grad_out_a, grad_in_b, rank_local), 'tok')  86.5 us
    all_gather x1, waiting for transfers between devices, local(): in_rows = lax.all_gather(frozen_in, 'tok', axis=0, tiled=True)  80.7 us
    all_gather x1, waiting for transfers between devices, local(): lax.all_gather(frozen_out, 'tok', axis=1, tiled=True)  69.7 us
    reduce_scatter x1, waiting for transfers between devices, local(): lax.psum_scatter(dx_term, 'hid', scatter_dimension=1, tiled=True)  41.8 us
    reduce_scatter x1, waiting for transfers between devices, local(): lax.psum_scatter(rank_terms, 'hid', scatter_dimension=1, tiled=True)  27.9 us
    all_gather x1, waiting for transfers between devices, local(): lax.all_gather(tokens, 'hid', axis=1, tiled=True)  23.7 us
    all_gather x1, waiting for transfers between devices, local(): lax.all_gather(cotangent, 'hid', axis=1, tiled=True)  15.1 us
    all_gather x1, blocking collectives, local(): in_a_full = lax.all_gather(input_adapter_first, 'hid', axis=0, tiled=True)  11 us
  transfers between devices with their start and end apart: 7, of which 7 were waited for; matrix products, arithmetic and copies ran while one was open for 7% of the time, Pallas kernels for 0%

commit v1 on v0

--- a/solution.py
+++ b/solution.py
@@ -7,6 +7,18 @@
 ADAPTER_SCALE = 0.5
 GELU_K = 0.7978845608
 GELU_C = 0.044715
+
+
+def collect(value, axis, dim):
+    ways, here, step = (lax.axis_size(axis), lax.axis_index(axis), value.shape[dim])
+    shape = [n * ways if d == dim else n for d, n in enumerate(value.shape)]
+    full = lax.dynamic_update_slice_in_dim(
+        jnp.zeros(shape, value.dtype), value, here * step, axis=dim
+    )
+    for far in range(1, ways):
+        value = lax.ppermute(value, axis, [(d, (d + 1) % ways) for d in range(ways)])
+        full = lax.dynamic_update_slice_in_dim(full, value, (here - far) % ways * step, axis=dim)
+    return full
 
 
 def gelu_pair(pre_activation):
@@ -35,7 +47,7 @@
     rank_width = input_adapter_second.shape[0]
     gradient_scale = ADAPTER_SCALE / math.sqrt(device_local_rows * lax.axis_size("tok"))
     full_tokens, full_cotan = (
-        lax.all_gather(tokens, "hid", axis=1, tiled=True),
+        collect(tokens, "hid", 1),
         lax.all_gather(cotangent, "hid", axis=1, tiled=True),
     )
     in_rows = lax.all_gather(frozen_in, "tok", axis=0, tiled=True)

time: 422 us -> 399 us (0.945)
  waiting for transfers between devices: 348 us -> 320 us
    ppermute x0 -> x7, waiting for transfers between devices: none -> 31.6 us  [collect(): lax.ppermute(value, axis, [(d, (d + 1) % ways) for d in range(ways)])]
    all_gather x1 -> x0, waiting for transfers between devices: 23.7 us -> none  [local(): lax.all_gather(tokens, 'hid', axis=1, tiled=True)]
    all_gather x1, waiting for transfers between devices: 15.1 us -> 0.01 us  [local(): lax.all_gather(cotangent, 'hid', axis=1, tiled=True)]
    all_gather x1, waiting for transfers between devices: 69.7 us -> 58.7 us  [local(): lax.all_gather(frozen_out, 'tok', axis=1, tiled=True)]
    all_gather x1, waiting for transfers between devices: 80.7 us -> 73.7 us  [local(): in_rows = lax.all_gather(frozen_in, 'tok', axis=0, tiled=True)]
  transfers between devices with their start and end apart: 7 -> 13, of which waited for: 7 -> 11; matrix products, arithmetic and copies ran while one was open for 7% -> 8% of each run, Pallas kernels for 0% -> 0%
where the time goes in v1:
time: 399 us
  waiting for transfers between devices  320 us (80%)
  matrix products  42.9 us (11%)
  between operations  14.4 us (4%)
  blocking collectives  11.1 us (3%)
  local copies, waits for them, and re-layouts  6.66 us (2%)
    psum x1, waiting for transfers between devices, local(): lax.psum((grad_out_a, grad_in_b, rank_local), 'tok')  86.5 us
    all_gather x1, waiting for transfers between devices, local(): in_rows = lax.all_gather(frozen_in, 'tok', axis=0, tiled=True)  73.7 us
    all_gather x1, waiting for transfers between devices, local(): lax.all_gather(frozen_out, 'tok', axis=1, tiled=True)  58.7 us
    reduce_scatter x1, waiting for transfers between devices, local(): lax.psum_scatter(dx_term, 'hid', scatter_dimension=1, tiled=True)  41.7 us
    ppermute x7, waiting for transfers between devices, collect(): lax.ppermute(value, axis, [(d, (d + 1) % ways) for d in range(ways)])  31.6 us
    reduce_scatter x1, waiting for transfers between devices, local(): lax.psum_scatter(rank_terms, 'hid', scatter_dimension=1, tiled=True)  25.7 us
    all_gather x1, blocking collectives, local(): in_a_full = lax.all_gather(input_adapter_first, 'hid', axis=0, tiled=True)  11.1 us
  transfers between devices with their start and end apart: 13, of which 11 were waited for; matrix products, arithmetic and copies ran while one was open for 8% of the time, Pallas kernels for 0%

profile of v1, /device:TPU:0, one launch (start us, length us, event | category | flops | bytes accessed | tf_op | source)
XLA Modules:
  0.0 398.8 jit_solution(3100576399033958593)
XLA Ops:
  7.2 0.0 copy-start
  7.2 0.0 all-gather.4.cloned.1.call-start
  7.2 0.7 all-gather.4.cloned.1.call-update
  7.9 0.0 all-gather.6.cloned.1.call-start
  8.0 0.7 all-gather.6.cloned.1.call-update
  8.7 0.0 all-gather.8.cloned.1.call-start
  8.7 0.7 all-gather.8.cloned.1.call-update
  9.4 0.0 reduce-scatter.5.cloned.1.call-start
  9.4 0.5 collective-permute-start
  10.0 5.7 %collective-permute-done = bf16[512,128]{1,0:T(8,128)(2,1)S(1)} collective-permute-done((bf16[512,128]{1,0:T(8,128)(2,1)}, bf16[512,128]{1,0:T(8,128)(2,1)S(1)}, u32[]{:S(2)}, u32[]{:S(2)}) %collective-permute-start) | collective-permute-done | bytes 131104 | tf_op jit(solution)/shard_map/ppermute | solution.py:19
  15.7 5.3 %collective-permute-done.1 = bf16[512,128]{1,0:T(8,128)(2,1)S(1)} collective-permute-done((bf16[512,128]{1,0:T(8,128)(2,1)S(1)}, bf16[512,128]{1,0:T(8,128)(2,1)S(1)}, u32[]{:S(2)}, u32[]{:S(2)}) %collective-permute-start.1) | collective-permute-done | bytes 131104 | tf_op jit(solution)/shard_map/ppermute | solution.py:19
  21.0 5.3 %collective-permute-done.2 = bf16[512,128]{1,0:T(8,128)(2,1)S(1)} collective-permute-done((bf16[512,128]{1,0:T(8,128)(2,1)S(1)}, bf16[512,128]{1,0:T(8,128)(2,1)S(1)}, u32[]{:S(2)}, u32[]{:S(2)}) %collective-permute-start.2) | collective-permute-done | bytes 131104 | tf_op jit(solution)/shard_map/ppermute | solution.py:19
  26.3 11.1 %all_gather.15 = bf16[1024,128]{1,0:T(8,128)(2,1)S(1)} all-gather(bf16[128,128]{1,0:T(8,128)(2,1)} %param.12), channel_id=1, replica_groups=mesh['tok'=4,'hid'=8] {'hid'}, dimensions={0}, use_global_device_ids=true | all-gather | bytes 294912 | tf_op jit(solution)/shard_map/all_gather | solution.py:54
  37.4 0.1 broadcast_in_dim.3
  37.6 0.9 constant_dynamic-update-slice_fusion.7
  38.6 0.4 collective-permute-start.4
  39.0 4.9 %collective-permute-done.4 = bf16[512,128]{1,0:T(8,128)(2,1)S(1)} collective-permute-done((bf16[512,128]{1,0:T(8,128)(2,1)S(1)}, bf16[512,128]{1,0:T(8,128)(2,1)S(1)}, u32[]{:S(2)}, u32[]{:S(2)}) %collective-permute-start.4) | collective-permute-done | bytes 131104 | tf_op jit(solution)/shard_map/ppermute | solution.py:19
  44.0 5.2 %collective-permute-done.5 = bf16[512,128]{1,0:T(8,128)(2,1)S(1)} collective-permute-done((bf16[512,128]{1,0:T(8,128)(2,1)S(1)}, bf16[512,128]{1,0:T(8,128)(2,1)S(1)}, u32[]{:S(2)}, u32[]{:S(2)}) %collective-permute-start.5) | collective-permute-done | bytes 131104 | tf_op jit(solution)/shard_map/ppermute | solution.py:19
  49.3 5.2 %collective-permute-done.6 = bf16[512,128]{1,0:T(8,128)(2,1)S(1)} collective-permute-done((bf16[512,128]{1,0:T(8,128)(2,1)S(1)}, bf16[512,128]{1,0:T(8,128)(2,1)S(1)}, u32[]{:S(2)}, u32[]{:S(2)}) %collective-permute-start.6) | collective-permute-done | bytes 131104 | tf_op jit(solution)/shard_map/ppermute | solution.py:19
  54.5 0.4 fusion.10
  55.0 3.7 fusion.11
  58.7 1.7 fusion.9
  60.4 58.7 %all-gather.6.cloned.1.call-done = bf16[2048,1024]{1,0:T(8,128)(2,1)} async-done(((bf16[2048,256]{1,0:T(8,128)(2,1)}), bf16[2048,1024]{1,0:T(8,128)(2,1)}) %all-gather.6.cloned.1.call-update) | async-done | bytes 4194320 | tf_op jit(solution)/shard_map/all_gather | solution.py:70
  119.1 6.9 %fusion.8 = f32[512,2048]{1,0:T(8,128)} fusion(bf16[512,1024]{1,0:T(8,128)(2,1)} %all-gather.4.cloned.1.call-done, bf16[2048,1024]{1,0:T(8,128)(2,1)} %all-gather.6.cloned.1.call-done), kind=kOutput, calls=%fused_computation.26 | convolution fusion | flops 2147483648 | bytes 9437184 | tf_op jit(solution)/shard_map/td,fd->tf/dot_general | solution.py:67
  125.9 73.7 %all-gather.8.cloned.1.call-done = bf16[1024,2048]{1,0:T(8,128)(2,1)} async-done(((bf16[256,2048]{1,0:T(8,128)(2,1)}), bf16[1024,2048]{1,0:T(8,128)(2,1)}) %all-gather.8.cloned.1.call-update) | async-done | bytes 4194320 | tf_op jit(solution)/shard_map/all_gather | solution.py:53
  199.6 7.0 %multiply_convert_fusion = (bf16[512,2048]{1,0:T(8,128)(2,1)S(1)}, f32[512,2048]{1,0:T(8,128)S(1)}) fusion(f32[512,2048]{1,0:T(8,128)} %fusion.11, bf16[512,1024]{1,0:T(8,128)(2,1)S(1)} %constant_dynamic-update-slice_fusion, bf16[1024,2048]{1,0:T(8,128)(2,1)} %all-gather.8.cloned.1.call-done), kind=kOutput, calls=%fused_computation.9 | convolution fusion | flops 2159017984 | bytes 15728640 | tf_op jit(solution)/shard_map/dot_general | solution.py:58
  206.6 4.9 %fusion.6 = bf16[512,2048]{1,0:T(8,128)(2,1)S(1)} fusion(f32[512,2048]{1,0:T(8,128)S(1)} %get-tuple-element.16, f32[512,2048]{1,0:T(8,128)S(1)} %copy-done.8, f32[512,128]{1,0:T(8,128)S(1)} %fusion.9, bf16[2048,128]{1,0:T(8,128)(2,1)S(1)} %copy-done.6), kind=kOutput, calls=%fused_computation.8 | convolution fusion | flops 1632632832 | bytes 11272192 | tf_op jit(solution)/shard_map/dot_general | solution.py:73
  211.5 0.7 fusion.13
  212.3 0.7 fusion.16
  212.9 0.7 fusion.14
  213.7 0.7 fusion.15
  214.3 1.0 pad_maximum_fusion
  215.4 0.0 reduce-scatter.5.cloned.1.call-update
  215.4 0.2 all-reduce.3.cloned.1.call-start
  215.6 3.7 convolution_multiply_fusion.1
  219.4 5.0 %convolution_multiply_fusion = f32[2048,128]{1,0:T(8,128)} fusion(bf16[512,2048]{1,0:T(8,128)(2,1)} %copy-done.3, f32[512,128]{1,0:T(8,128)} %copy-done.5), kind=kOutput, calls=%fused_computation.11 | convolution fusion | flops 1610874880 | bytes 3407872 | tf_op jit(solution)/shard_map/dot_general | solution.py:81
  224.3 25.7 %reduce-scatter.5.cloned.1.call-done = f32[256,128]{1,0:T(8,128)} async-done(((f32[256,1024]{1,0:T(8,128)}), f32[256,128]{1,0:T(8,128)}) %reduce-scatter.5.cloned.1.call-update) | async-done | bytes 131088 | tf_op jit(solution)/shard_map/reduce_scatter | solution.py:96
  250.0 0.0 all-reduce.3.cloned.1.call-update
  250.0 0.0 reduce-scatter.3.cloned.1.call-start
  250.1 4.5 %fusion.12 = f32[512,1024]{1,0:T(8,128)S(1)} fusion(bf16[512,2048]{1,0:T(8,128)(2,1)S(1)} %copy-done.2, bf16[1024,2048]{1,0:T(8,128)(2,1)} %all-gather.8.cloned.1.call-done), kind=kOutput, calls=%fused_computation.30 | convolution fusion | flops 2147483648 | bytes 8388608 | tf_op jit(solution)/shard_map/tf,df->td/dot_general | solution.py:80
  254.6 2.4 multiply_add_fusion.2
  257.0 0.0 reduce-scatter.3.cloned.1.call-update
  257.0 86.5 %all-reduce.3.cloned.1.call-done = (f32[256,128]{1,0:T(8,128)}, f32[128,2048]{1,0:T(8,128)}, f32[2048,128]{1,0:T(8,128)}) async-done(((f32[256,128]{1,0:T(8,128)}, f32[128,2048]{1,0:T(8,128)}, f32[2048,128]{1,0:T(8,128)}), (f32[256,128]{1,0:T(8,128)}, f32[128,2048]{1,0:T(8,128)}, f32[2048,128]{1,0:T(8,128)})) %all-reduce.3.cloned.1.call-update) | async-done | bytes 2228240 | tf_op jit(solution)/shard_map/psum | solution.py:98
  343.5 1.5 slice_multiply_fusion
  345.0 0.7 copy.13
  345.7 41.7 %reduce-scatter.3.cloned.1.call-done = f32[512,128]{1,0:T(8,128)} async-done(((f32[512,1024]{1,0:T(8,128)}), f32[512,128]{1,0:T(8,128)}) %reduce-scatter.3.cloned.1.call-update) | async-done | bytes 262160 | tf_op jit(solution)/shard_map/reduce_scatter | solution.py:95
  387.4 2.3 copy.25
  389.7 2.3 copy.26
  (31 shorter events, 0.3 us)
Async XLA Ops:
  7.2 47.8 %copy-start = (bf16[128,2048]{1,0:T(8,128)(2,1)S(1)}, bf16[128,2048]{1,0:T(8,128)(2,1)}, u32[]{:S(2)}) copy-start(bf16[128,2048]{1,0:T(8,128)(2,1)} %param.13) | copy-start | bytes 1572868
  7.2 51.5 %all-gather.4.cloned.1.call-start = ((), (), s32[]{:S(2)}) async-start(), calls=%async_computation.2 | async-start | bytes 1179648 | tf_op jit(solution)/shard_map/all_gather | solution.py:51
  7.9 111.2 %all-gather.6.cloned.1.call-start = ((), (), s32[]{:S(2)}) async-start(), calls=%async_computation.3 | async-start | bytes 5242880 | tf_op jit(solution)/shard_map/all_gather | solution.py:70
  8.7 190.9 %all-gather.8.cloned.1.call-start = ((), (), s32[]{:S(2)}) async-start(), calls=%async_computation.4 | async-start | bytes 5242880 | tf_op jit(solution)/shard_map/all_gather | solution.py:53
  9.4 240.6 %reduce-scatter.5.cloned.1.call-start = ((), (), s32[]{:S(2)}) async-start(), calls=%async_computation.6 | async-start | bytes 1179648 | tf_op jit(solution)/shard_map/reduce_scatter | solution.py:96
  9.4 6.3 %collective-permute-start = (bf16[512,128]{1,0:T(8,128)(2,1)}, bf16[512,128]{1,0:T(8,128)(2,1)S(1)}, u32[]{:S(2)}, u32[]{:S(2)}) collective-permute-start(bf16[512,128]{1,0:T(8,128)(2,1)} %param.8), channel_id=1, source_target_pairs={{0,1},{1,2},{2,3},{3,4},{4,5},{5,6},{6,7},{7,0},{8,9},{9,10},{10,1... | collective-permute-start | bytes 393224 | tf_op jit(solution)/shard_map/ppermute | solution.py:19
  15.7 5.3 %collective-permute-start.1 = (bf16[512,128]{1,0:T(8,128)(2,1)S(1)}, bf16[512,128]{1,0:T(8,128)(2,1)S(1)}, u32[]{:S(2)}, u32[]{:S(2)}) collective-permute-start(bf16[512,128]{1,0:T(8,128)(2,1)S(1)} %collective-permute-done), channel_id=1, source_target_pairs={{0,1},{1,2},{2,3},{3,4},{4,5},{5,6},{6,7},{7,0},{8,9},{9,10},{10,1... | collective-permute-start | bytes 393224 | tf_op jit(solution)/shard_map/ppermute | solution.py:19
  21.0 5.3 %collective-permute-start.2 = (bf16[512,128]{1,0:T(8,128)(2,1)S(1)}, bf16[512,128]{1,0:T(8,128)(2,1)S(1)}, u32[]{:S(2)}, u32[]{:S(2)}) collective-permute-start(bf16[512,128]{1,0:T(8,128)(2,1)S(1)} %collective-permute-done.1), channel_id=1, source_target_pairs={{0,1},{1,2},{2,3},{3,4},{4,5},{5,6},{6,7},{7,0},{8,9},{9,10},{10,1... | collective-permute-start | bytes 393224 | tf_op jit(solution)/shard_map/ppermute | solution.py:19
  26.3 12.2 %collective-permute-start.3 = (bf16[512,128]{1,0:T(8,128)(2,1)S(1)}, bf16[512,128]{1,0:T(8,128)(2,1)S(1)}, u32[]{:S(2)}, u32[]{:S(2)}) collective-permute-start(bf16[512,128]{1,0:T(8,128)(2,1)S(1)} %collective-permute-done.2), channel_id=1, source_target_pairs={{0,1},{1,2},{2,3},{3,4},{4,5},{5,6},{6,7},{7,0},{8,9},{9,10},{10,1... | collective-permute-start | bytes 393224 | tf_op jit(solution)/shard_map/ppermute | solution.py:19
  38.5 20.2 %copy-start.7 = (bf16[128,1024]{1,0:T(8,128)(2,1)S(1)}, bf16[128,1024]{1,0:T(8,128)(2,1)}, u32[]{:S(2)}) copy-start(bf16[128,1024]{1,0:T(8,128)(2,1)} %param.15) | copy-start | bytes 786436
  38.6 5.3 %collective-permute-start.4 = (bf16[512,128]{1,0:T(8,128)(2,1)S(1)}, bf16[512,128]{1,0:T(8,128)(2,1)S(1)}, u32[]{:S(2)}, u32[]{:S(2)}) collective-permute-start(bf16[512,128]{1,0:T(8,128)(2,1)S(1)} %collective-permute-done.3), channel_id=1, source_target_pairs={{0,1},{1,2},{2,3},{3,4},{4,5},{5,6},{6,7},{7,0},{8,9},{9,10},{10,1... | collective-permute-start | bytes 393224 | tf_op jit(solution)/shard_map/ppermute | solution.py:19
  43.9 5.3 %collective-permute-start.5 = (bf16[512,128]{1,0:T(8,128)(2,1)S(1)}, bf16[512,128]{1,0:T(8,128)(2,1)S(1)}, u32[]{:S(2)}, u32[]{:S(2)}) collective-permute-start(bf16[512,128]{1,0:T(8,128)(2,1)S(1)} %collective-permute-done.4), channel_id=1, source_target_pairs={{0,1},{1,2},{2,3},{3,4},{4,5},{5,6},{6,7},{7,0},{8,9},{9,10},{10,1... | collective-permute-start | bytes 393224 | tf_op jit(solution)/shard_map/ppermute | solution.py:19
  49.2 5.3 %collective-permute-start.6 = (bf16[512,128]{1,0:T(8,128)(2,1)S(1)}, bf16[512,128]{1,0:T(8,128)(2,1)S(1)}, u32[]{:S(2)}, u32[]{:S(2)}) collective-permute-start(bf16[512,128]{1,0:T(8,128)(2,1)S(1)} %collective-permute-done.5), channel_id=1, source_target_pairs={{0,1},{1,2},{2,3},{3,4},{4,5},{5,6},{6,7},{7,0},{8,9},{9,10},{10,1... | collective-permute-start | bytes 393224 | tf_op jit(solution)/shard_map/ppermute | solution.py:19
  60.4 146.2 %copy-start.5 = (f32[512,128]{1,0:T(8,128)}, f32[512,128]{1,0:T(8,128)S(1)}, u32[]{:S(2)}) copy-start(f32[512,128]{1,0:T(8,128)S(1)} %fusion.9) | copy-start | bytes 786436
  125.9 80.7 %copy-start.6 = (bf16[2048,128]{1,0:T(8,128)(2,1)S(1)}, bf16[2048,128]{1,0:T(8,128)(2,1)}, u32[]{:S(2)}) copy-start(bf16[2048,128]{1,0:T(8,128)(2,1)} %param.14) | copy-start | bytes 1572868
  199.6 7.0 %copy-start.8 = (f32[512,2048]{1,0:T(8,128)S(1)}, f32[512,2048]{1,0:T(8,128)}, u32[]{:S(2)}) copy-start(f32[512,2048]{1,0:T(8,128)} %fusion.8) | copy-start | bytes 12582916
  206.6 6.3 %copy-start.3 = (bf16[512,2048]{1,0:T(8,128)(2,1)}, bf16[512,2048]{1,0:T(8,128)(2,1)S(1)}, u32[]{:S(2)}) copy-start(bf16[512,2048]{1,0:T(8,128)(2,1)S(1)} %get-tuple-element.15) | copy-start | bytes 6291460
  211.5 2.8 copy-start.1
  211.5 2.1 copy-start.4
  215.4 34.7 %copy-start.2 = (bf16[512,2048]{1,0:T(8,128)(2,1)S(1)}, bf16[512,2048]{1,0:T(8,128)(2,1)}, u32[]{:S(2)}) copy-start(bf16[512,2048]{1,0:T(8,128)(2,1)} %copy-done.1) | copy-start | bytes 6291460
  215.4 128.1 %all-reduce.3.cloned.1.call-start = ((), (), s32[]{:S(2)}) async-start(), calls=%async_computation.7 | async-start | bytes 4456448 | tf_op jit(solution)/shard_map/psum | solution.py:98
  250.0 137.4 %reduce-scatter.3.cloned.1.call-start = ((), (), s32[]{:S(2)}) async-start(), calls=%async_computation.5 | async-start | bytes 2359296 | tf_op jit(solution)/shard_map/reduce_scatter | solution.py:95
Sparse Core Ops, SparseCore 0:
  9.9 27.2 all-gather.3
  38.7 80.3 all-gather.5
  120.6 78.9 all-gather.7
  215.5 34.4 reduce-scatter.4
  253.0 90.4 all-reduce.2
  347.2 40.1 reduce-scatter.2
